TPU v7x, 256 devices: a whole 4x4x8 slice. The times are simulated.
256 devices in a mesh: row: 8 (over z_hi, core), col: 32 (over y, x, z_lo).
Axes of the slice: x: 4, y: 4, z: 8 (z_hi: 4, z_lo: 2; z = z_hi * 2 + z_lo), core: 2. Of those that a mesh axis runs over, the one named last changes fastest.
Arguments:
- features: bfloat16 [65536, 256], P(('row', 'col')), may hold values from -6 to 6
- layer_weight: bfloat16 [256, 256], replicated, may hold values from -0.375 to 0.375
- layer_bias: float32 [256], replicated, may hold values from -3 to 3
- cotangent: bfloat16 [65536, 256], P(('row', 'col')), may hold values from -6 to 6
- tile_values: bfloat16 [8192, 256, 256], P(('row', 'col')), may hold values from -0.0625 to 0.0625
- tile_index: int32 [8192, 2], P(('row', 'col')), may hold values from -1 to 255, as said below
Outputs:
- activations: bfloat16 [65536, 256], P(('row', 'col'))
- node_grad: bfloat16 [65536, 256], P(('row', 'col'))
- weight_grad: float32 [256, 256], P(('row', 'col'))
- bias_grad: float32 [256], P(('row', 'col'))
Inputs may be any that keep to these rules, and one draw needn't show every extreme that they name: `tile_index`: each pair is (I, J) with I <= J; device r * 32 + c holds only pairs whose I lies in blocks r * 32 * 1 to (r + 1) * 32 - 1 and whose J // 1 equals c modulo 32. Each pair is held by at most one slot among all devices. A device's live slots come first, its empty slots hold -1 in both entries; counts differ from device to device, and some device fills all 32 slots.
All inputs are finite; a program needn't handle non-finite values.
Results may differ from a plain program's by a relative error of at most 0.025.
Values may be sent and summed in bfloat16 or wider, within the bound.
No kernel may reach another device: no remote copies, remote signals or barrier semaphores. Data moves between devices by JAX's collectives and lax.ppermute only.
A program may use at most 128 MiB of HBM per device.

v0:
```python
import jax
import jax.numpy as jnp
from jax import lax
from jax.sharding import Mesh
from jax.sharding import PartitionSpec as P

BLK_DEV = 1
ROW = ("row_0", "row_1")
ROW_COL = ("row_0", "row_1", "col")


def laid_out(blocks, dim):
    blocks = jnp.moveaxis(blocks, 0, dim)
    shape = blocks.shape
    return blocks.reshape(*shape[:dim], shape[dim] * shape[dim + 1], *shape[dim + 2 :])


def stacked_from(array, axes, sequence):
    blocks = array[None]
    for k in sequence:
        blocks = lax.all_gather(blocks, axes[k], axis=0, tiled=True)
    current = [lax.axis_size(axes[k]) for k in reversed(sequence)]
    blocks = blocks.reshape(*current, *array.shape)
    turned = sorted(range(len(sequence)), key=lambda place: sequence[len(sequence) - 1 - place])
    return blocks.transpose(*turned, *range(len(sequence), blocks.ndim)).reshape(-1, *array.shape)


def gathered_by_axis(array, axes, sequence, dim):
    return laid_out(stacked_from(array, axes, sequence), dim)


def split_up(array, dim, length):
    shape = array.shape
    blocks = array.reshape(*shape[:dim], length, shape[dim] // length, *shape[dim + 1 :])
    return jnp.moveaxis(blocks, dim, 0)


def sent_and_summed(array, axis, dim):
    length = lax.axis_size(axis)
    blocks = lax.all_to_all(split_up(array, dim, length), axis, 0, 0, tiled=True)
    return jnp.sum(blocks.astype(jnp.float32), axis=0)


def sum_in_order(blocks, axes, sequence):
    shape = [lax.axis_size(a) for a in axes]
    blocks = blocks.reshape(*shape, *blocks.shape[1:])
    blocks = blocks.transpose(*sequence, *range(len(axes), blocks.ndim))
    blocks = blocks.reshape(-1, *blocks.shape[len(axes) :])
    for k in sequence:
        blocks = lax.psum_scatter(blocks, axes[k], scatter_dimension=0, tiled=True)
    return blocks[0]


def summed_rows(array, axes, sequence, dim):
    length = lax.axis_size(axes)
    return sum_in_order(split_up(array, dim, length), axes, sequence)


def aggregate(node_data, tile_values, tile_index):
    tile_size = tile_values.shape[1]
    feature_count = node_data.shape[1]
    column_devices = lax.axis_size("col")
    row_index = lax.axis_index(ROW)
    column_group = gathered_by_axis(node_data, ROW, (0, 1), 0)
    row_group = lax.all_gather(node_data, "col", axis=0, tiled=True)
    column_blocks = column_group.reshape(-1, tile_size, feature_count)
    row_blocks = row_group.reshape(-1, tile_size, feature_count)
    row_span = row_blocks.shape[0]
    column_span = column_blocks.shape[0]
    block_row = tile_index[:, 0]
    block_column = tile_index[:, 1]
    occupied = block_row >= 0
    row_slot = jnp.where(occupied, block_row - row_index * row_span, 0)
    column_slot = jnp.where(
        occupied, block_column // BLK_DEV // column_devices * BLK_DEV + block_column % BLK_DEV, 0
    )
    column_inputs = jnp.take(column_blocks, column_slot, axis=0)
    row_inputs = jnp.take(row_blocks, row_slot, axis=0)
    forward_terms = jnp.einsum(
        "tnm,tmf->tnf", tile_values, column_inputs, preferred_element_type=jnp.float32
    )
    mirror_terms = jnp.einsum(
        "tmn,tmf->tnf", tile_values, row_inputs, preferred_element_type=jnp.float32
    )
    live = occupied.astype(jnp.float32)[:, None, None]
    row_partial = (
        jnp.zeros((row_span, tile_size, feature_count), jnp.float32)
        .at[row_slot]
        .add(forward_terms * live)
    )
    column_partial = (
        jnp.zeros((column_span, tile_size, feature_count), jnp.float32)
        .at[column_slot]
        .add(mirror_terms * live)
    )
    row_partial = row_partial.reshape(row_span * tile_size, feature_count)
    column_partial = column_partial.reshape(column_span * tile_size, feature_count)
    row_sums = sent_and_summed(row_partial.astype(jnp.bfloat16), "col", 0)
    column_sums = summed_rows(column_partial.astype(jnp.bfloat16), ROW, (1, 0), 0).astype(
        jnp.float32
    )
    return (row_sums + column_sums).astype(jnp.bfloat16)


def local(features, layer_weight, layer_bias, cotangent, tile_values, tile_index):
    aggregated = aggregate(features, tile_values, tile_index)
    hidden = jnp.dot(aggregated, layer_weight, preferred_element_type=jnp.float32) + layer_bias
    logistic = jax.nn.sigmoid(hidden)
    activations = (hidden * logistic).astype(jnp.bfloat16)
    derivative = logistic * (1.0 + hidden * (1.0 - logistic))
    hidden_grad = (cotangent.astype(jnp.float32) * derivative).astype(jnp.bfloat16)
    message_grad = jnp.dot(hidden_grad, layer_weight.T, preferred_element_type=jnp.float32).astype(
        jnp.bfloat16
    )
    total_nodes = features.shape[0] * lax.axis_size(ROW) * lax.axis_size("col")
    grad_scale = total_nodes ** (-0.5)
    weight_part = (
        lax.dot_general(
            aggregated, hidden_grad, (((0,), (0,)), ((), ())), preferred_element_type=jnp.float32
        )
        * grad_scale
    )
    bias_part = jnp.sum(hidden_grad.astype(jnp.float32), axis=0) * grad_scale
    weight_grad, bias_grad = (
        lax.psum_scatter(weight_part, ROW_COL, scatter_dimension=0, tiled=True),
        lax.psum_scatter(bias_part, ROW_COL, scatter_dimension=0, tiled=True),
    )
    node_grad = aggregate(message_grad, tile_values, tile_index)
    return (activations, node_grad, weight_grad, bias_grad)


def solution(mesh):
    split = Mesh(mesh.devices.reshape(4, 2, mesh.shape["col"]), ("row_0", "row_1", "col"))
    in_specs = (
        P(ROW_COL, None),
        P(),
        P(),
        P(ROW_COL, None),
        P(ROW_COL, None, None),
        P(ROW_COL, None),
    )
    out_specs = (P(ROW_COL, None), P(ROW_COL, None), P(ROW_COL, None), P(ROW_COL))
    return jax.shard_map(local, mesh=split, in_specs=in_specs, out_specs=out_specs, check_vma=False)
```

profile of v0, /device:TPU:8, one launch (start us, length us, event | category | flops | bytes accessed | tf_op | source)
XLA Modules:
  0.0 879.9 jit_solution(5137925944958161656)
XLA Ops:
  7.2 20.7 %all-gather = bf16[1024,256]{1,0:T(8,128)(2,1)} all-gather(bf16[256,256]{1,0:T(8,128)(2,1)} %param.10), channel_id=2, replica_groups=mesh['row_0'=4,'row_1'=2,'col'=32] {'row_0'}, dimensions={0}, use_global_device_ids=true | all-gather | bytes 655360 | tf_op jit(solution)/shard_map/all_gather | solution.py:21
  30.9 11.1 %all-gather.7.cloned.1.call-done = bf16[8,256,256]{2,1,0:T(8,128)(2,1)} async-done(((bf16[4,256,256]{2,1,0:T(8,128)(2,1)}), bf16[8,256,256]{2,1,0:T(8,128)(2,1)}) %all-gather.7.cloned.1.call-update) | async-done | bytes 1048592 | tf_op jit(solution)/shard_map/all_gather | solution.py:21
  46.1 8.7 multiply_bitcast_fusion.3
  54.8 9.0 %copy.39 = f32[32,256,256]{2,1,0:T(8,128)} copy(f32[32,256,256]{1,2,0:T(8,128)} %multiply_bitcast_fusion.3) | data formatting | bytes 16777216 | tf_op jit(solution)/shard_map/mul | solution.py:89
  63.8 4.2 broadcast.111.clone
  67.9 18.3 %scatter_fusion = f32[32,256,256]{2,1,0:T(8,128)} fusion(f32[32,256,256]{2,1,0:T(8,128)} %broadcast.111.clone, s32[32]{0:T(128)S(1)} %get-tuple-element.16, f32[32,256,256]{2,1,0:T(8,128)} %copy.39), kind=kCustom, calls=%fused_computation.4 | custom fusion | flops 2097152 | bytes 25165952 | tf_op jit(solution)/shard_map/scatter-add | solution.py:89
  86.2 5.9 convert_element_type.70
  92.2 8.4 all-to-all-start
  100.6 122.7 %all-gather.9.cloned.1.call-done = bf16[8192,256]{1,0:T(8,128)(2,1)} async-done(((bf16[256,256]{1,0:T(8,128)(2,1)}), bf16[8192,256]{1,0:T(8,128)(2,1)}) %all-gather.9.cloned.1.call-update) | async-done | bytes 4194320 | tf_op jit(solution)/shard_map/all_gather | solution.py:65
  223.4 5.0 gather_fusion.1
  228.3 8.6 multiply_bitcast_fusion.2
  236.9 9.0 %copy.41 = f32[32,256,256]{2,1,0:T(8,128)} copy(f32[32,256,256]{1,2,0:T(8,128)} %multiply_bitcast_fusion.2) | data formatting | bytes 16777216 | tf_op jit(solution)/shard_map/mul | solution.py:94
  246.1 11.6 %scatter_fusion.1 = f32[8,256,256]{2,1,0:T(8,128)S(1)} fusion(f32[8,256,256]{2,1,0:T(8,128)S(1)} %broadcast.114.clone, s32[32]{0:T(128)S(1)} %get-tuple-element.15, f32[32,256,256]{2,1,0:T(8,128)} %copy.41), kind=kCustom, calls=%fused_computation.5 | custom fusion | flops 2097152 | bytes 25165952 | tf_op jit(solution)/shard_map/scatter-add | solution.py:94
  259.0 23.5 %reduce-scatter.5.cloned.1.call-done = bf16[4,256,256]{2,1,0:T(8,128)(2,1)} async-done(((bf16[8,256,256]{2,1,0:T(8,128)(2,1)}), bf16[4,256,256]{2,1,0:T(8,128)(2,1)}) %reduce-scatter.5.cloned.1.call-update) | async-done | bytes 524304 | tf_op jit(solution)/shard_map/reduce_scatter | solution.py:50
  285.3 28.8 %reduce-scatter.7.cloned.1.call-done = bf16[1,256,256]{2,1,0:T(8,128)(2,1)} async-done(((bf16[4,256,256]{2,1,0:T(8,128)(2,1)}), bf16[1,256,256]{2,1,0:T(8,128)(2,1)}) %reduce-scatter.7.cloned.1.call-update) | async-done | bytes 131088 | tf_op jit(solution)/shard_map/reduce_scatter | solution.py:50
  316.3 17.2 %all-gather.1 = bf16[1024,256]{1,0:T(8,128)(2,1)} all-gather(bf16[256,256]{1,0:T(8,128)(2,1)S(1)} %convolution_convert_fusion), channel_id=3, replica_groups=mesh['row_0'=4,'row_1'=2,'col'=32] {'row_0'}, dimensions={0}, use_global_device_ids=true | all-gather | bytes 655360 | tf_op jit(solution)/shard_map/all_gather | solution.py:21
  334.0 12.4 %all-gather.11.cloned.1.call-done = bf16[8,256,256]{2,1,0:T(8,128)(2,1)} async-done(((bf16[4,256,256]{2,1,0:T(8,128)(2,1)}), bf16[8,256,256]{2,1,0:T(8,128)(2,1)}) %all-gather.11.cloned.1.call-update) | async-done | bytes 1048592 | tf_op jit(solution)/shard_map/all_gather | solution.py:21
  350.5 8.6 multiply_bitcast_fusion.1
  359.1 9.0 %copy.45 = f32[32,256,256]{2,1,0:T(8,128)} copy(f32[32,256,256]{1,2,0:T(8,128)} %multiply_bitcast_fusion.1) | data formatting | bytes 16777216 | tf_op jit(solution)/shard_map/mul | solution.py:89
  368.1 4.2 broadcast.111
  372.3 18.9 %scatter_fusion.2 = f32[32,256,256]{2,1,0:T(8,128)} fusion(f32[32,256,256]{2,1,0:T(8,128)} %broadcast.111, s32[32]{0:T(128)S(1)} %get-tuple-element.16, f32[32,256,256]{2,1,0:T(8,128)} %copy.45), kind=kCustom, calls=%fused_computation.6 | custom fusion | flops 2097152 | bytes 25165952 | tf_op jit(solution)/shard_map/scatter-add | solution.py:89
  391.2 5.9 convert_element_type.81
  397.1 8.4 all-to-all-start.1
  405.6 121.7 %all-gather.13.cloned.1.call-done = bf16[8192,256]{1,0:T(8,128)(2,1)} async-done(((bf16[256,256]{1,0:T(8,128)(2,1)}), bf16[8192,256]{1,0:T(8,128)(2,1)}) %all-gather.13.cloned.1.call-update) | async-done | bytes 4194320 | tf_op jit(solution)/shard_map/all_gather | solution.py:65
  527.3 4.9 gather_fusion.3
  532.2 8.6 multiply_bitcast_fusion
  540.9 9.0 %copy.47 = f32[32,256,256]{2,1,0:T(8,128)} copy(f32[32,256,256]{1,2,0:T(8,128)} %multiply_bitcast_fusion) | data formatting | bytes 16777216 | tf_op jit(solution)/shard_map/mul | solution.py:94
  550.0 11.6 %scatter_fusion.3 = f32[8,256,256]{2,1,0:T(8,128)S(1)} fusion(f32[8,256,256]{2,1,0:T(8,128)S(1)} %broadcast.114, s32[32]{0:T(128)S(1)} %get-tuple-element.15, f32[32,256,256]{2,1,0:T(8,128)} %copy.47), kind=kCustom, calls=%fused_computation.7 | custom fusion | flops 2097152 | bytes 25165952 | tf_op jit(solution)/shard_map/scatter-add | solution.py:94
  563.9 21.4 %reduce-scatter.9.cloned.1.call-done = bf16[4,256,256]{2,1,0:T(8,128)(2,1)} async-done(((bf16[8,256,256]{2,1,0:T(8,128)(2,1)}), bf16[4,256,256]{2,1,0:T(8,128)(2,1)}) %reduce-scatter.9.cloned.1.call-update) | async-done | bytes 524304 | tf_op jit(solution)/shard_map/reduce_scatter | solution.py:50
  585.4 76.3 %all-reduce.1 = f32[256]{0:T(256)S(1)} all-reduce(f32[256]{0:T(256)S(1)} %broadcast_multiply_fusion), channel_id=9, replica_groups=mesh['row_0'=4,'row_1'=2,'col'=32] {'row_0','row_1','col'}, use_global_device_ids=true, to_apply=%region_12.15.clone | all-reduce | flops 256 | bytes 2048
  662.3 180.3 %all-reduce.4.cloned.1.call-done = f32[256,256]{1,0:T(8,128)} async-done(((f32[256,256]{1,0:T(8,128)}), f32[256,256]{1,0:T(8,128)}) %all-reduce.4.cloned.1.call-update) | async-done | bytes 262160
  846.6 25.2 %reduce-scatter.11.cloned.1.call-done = bf16[1,256,256]{2,1,0:T(8,128)(2,1)} async-done(((bf16[4,256,256]{2,1,0:T(8,128)(2,1)}), bf16[1,256,256]{2,1,0:T(8,128)(2,1)}) %reduce-scatter.11.cloned.1.call-update) | async-done | bytes 131088 | tf_op jit(solution)/shard_map/reduce_scatter | solution.py:50
  (56 shorter events, 26.8 us)
Async XLA Ops:
  7.2 307.0 %copy-start = (bf16[256,256]{1,0:T(8,128)(2,1)S(1)}, bf16[256,256]{1,0:T(8,128)(2,1)}, u32[]{:S(2)}) copy-start(bf16[256,256]{1,0:T(8,128)(2,1)} %param.11) | copy-start | bytes 393220
  7.2 34.9 %all-gather.7.cloned.1.call-start = ((), (), s32[]{:S(2)}) async-start(), calls=%async_computation.6 | async-start | bytes 1572864 | tf_op jit(solution)/shard_map/all_gather | solution.py:21
  27.9 195.4 %all-gather.9.cloned.1.call-start = ((), (), s32[]{:S(2)}) async-start(), calls=%async_computation.7 | async-start | bytes 4325376 | tf_op jit(solution)/shard_map/all_gather | solution.py:65
  92.2 190.4 %all-to-all-start = ((bf16[32,256,256]{2,1,0:T(8,128)(2,1)}), bf16[32,256,256]{2,1,0:T(8,128)(2,1)}, u32[]{:S(2)}, u32[]{:S(2)}) async-start(bf16[32,256,256]{2,1,0:T(8,128)(2,1)} %convert_element_type.70), calls=%async_computation | async-start | bytes 8388608 | tf_op jit(solution)/shard_map/all_to_all | solution.py:40
  100.6 181.9 %reduce-scatter.5.cloned.1.call-start = ((), (), s32[]{:S(2)}) async-start(), calls=%async_computation.8 | async-start | bytes 1572864 | tf_op jit(solution)/shard_map/reduce_scatter | solution.py:50
  257.8 56.4 %copy-start.4 = (bf16[256,256]{1,0:T(8,128)(2,1)S(1)}, bf16[256,256]{1,0:T(8,128)(2,1)}, u32[]{:S(2)}) copy-start(bf16[256,256]{1,0:T(8,128)(2,1)} %param.13) | copy-start | bytes 393220
  257.8 56.4 %copy-start.5 = (f32[256]{0:T(256)S(1)}, f32[256]{0:T(256)}, u32[]{:S(2)}) copy-start(f32[256]{0:T(256)} %param.12) | copy-start | bytes 3076
  258.9 55.3 %reduce-scatter.7.cloned.1.call-start = ((), (), s32[]{:S(2)}) async-start(), calls=%async_computation.9 | async-start | bytes 655360 | tf_op jit(solution)/shard_map/reduce_scatter | solution.py:50
  282.5 64.0 %all-gather.11.cloned.1.call-start = ((), (), s32[]{:S(2)}) async-start(), calls=%async_computation.10 | async-start | bytes 1572864 | tf_op jit(solution)/shard_map/all_gather | solution.py:21
  316.3 17.4 %copy-start.2 = (bf16[256,256]{1,0:T(8,128)(2,1)}, bf16[256,256]{1,0:T(8,128)(2,1)S(1)}, u32[]{:S(2)}) copy-start(bf16[256,256]{1,0:T(8,128)(2,1)S(1)} %convolution_convert_fusion) | copy-start | bytes 393220
  333.5 193.8 %all-gather.13.cloned.1.call-start = ((), (), s32[]{:S(2)}) async-start(), calls=%async_computation.11 | async-start | bytes 4325376 | tf_op jit(solution)/shard_map/all_gather | solution.py:65
  397.1 446.7 %all-to-all-start.1 = ((bf16[32,256,256]{2,1,0:T(8,128)(2,1)}), bf16[32,256,256]{2,1,0:T(8,128)(2,1)}, u32[]{:S(2)}, u32[]{:S(2)}) async-start(bf16[32,256,256]{2,1,0:T(8,128)(2,1)} %convert_element_type.81), calls=%async_computation.3 | async-start | bytes 8388608 | tf_op jit(solution)/shard_map/all_to_all | solution.py:40
  405.6 179.8 %reduce-scatter.9.cloned.1.call-start = ((), (), s32[]{:S(2)}) async-start(), calls=%async_computation.12 | async-start | bytes 1572864 | tf_op jit(solution)/shard_map/reduce_scatter | solution.py:50
  561.6 1.3 copy-start.3
  561.8 311.6 %copy-start.1 = (bf16[256,256]{1,0:T(8,128)(2,1)S(1)}, bf16[256,256]{1,0:T(8,128)(2,1)}, u32[]{:S(2)}) copy-start(bf16[256,256]{1,0:T(8,128)(2,1)} %param.11) | copy-start | bytes 393220
  562.9 279.7 %all-reduce.4.cloned.1.call-start = ((), (), s32[]{:S(2)}) async-start(), calls=%async_computation.14 | async-start | bytes 524288
  563.9 307.9 %reduce-scatter.11.cloned.1.call-start = ((), (), s32[]{:S(2)}) async-start(), calls=%async_computation.13 | async-start | bytes 655360 | tf_op jit(solution)/shard_map/reduce_scatter | solution.py:50
Sparse Core Ops, SparseCore 0:
  28.1 13.9 all-gather.6
  43.8 179.4 all-gather.8
  259.0 23.3 reduce-scatter.4
  285.0 29.1 reduce-scatter.6
  333.6 12.8 all-gather.10
  348.8 178.3 all-gather.12
  563.0 22.3 reduce-scatter.8
  590.8 251.6 all-reduce.3
  845.1 26.6 reduce-scatter.10
where the time goes:
time: 882 us; the launch traced here: 880 us
  waiting for transfers between devices  548 us (62%)
  blocking collectives  114 us (13%)
  other arithmetic  81.9 us (9%)
  local copies, waits for them, and re-layouts  66.6 us (8%)
  matrix products  37.6 us (4%)
  starting transfers between devices  17.4 us (2%)
  between operations  14 us (2%)
    all_gather x2, waiting for transfers between devices, aggregate(): row_group = lax.all_gather(node_data, 'col', axis=0, tiled=True)  244 us
    unnamed x10, waiting for transfers between devices  181 us
    reduce_scatter x4, waiting for transfers between devices, sum_in_order(): blocks = lax.psum_scatter(blocks, axes[k], scatter_dimension=0, tiled=True)  99 us
    unnamed x1, blocking collectives  76.3 us
    all_gather x2, blocking collectives, stacked_from(): blocks = lax.all_gather(blocks, axes[k], axis=0, tiled=True)  37.8 us
    scatter-add x2, other arithmetic, aggregate(): row_partial = jnp.zeros((row_span, tile_size, feature_count), jnp.float32...  37.2 us
    all_gather x2, waiting for transfers between devices, stacked_from(): blocks = lax.all_gather(blocks, axes[k], axis=0, tiled=True)  23.5 us
    scatter-add x2, other arithmetic, aggregate(): column_partial = jnp.zeros((column_span, tile_size, feature_count), jnp.f...  23.3 us
  transfers between devices with their start and end apart: 11, of which 9 were waited for; matrix products, arithmetic and copies ran while one was open for 21% of the time, Pallas kernels for 0%

commit v1 on v0

--- a/solution.py
+++ b/solution.py
@@ -62,7 +62,12 @@
     column_devices = lax.axis_size("col")
     row_index = lax.axis_index(ROW)
     column_group = gathered_by_axis(node_data, ROW, (0, 1), 0)
-    row_group = lax.all_gather(node_data, "col", axis=0, tiled=True)
+    row_group = jnp.concatenate(
+        lax.all_to_all(
+            jnp.stack([node_data for _ in range(lax.axis_size("col"))], axis=0), "col", 0, 0
+        ),
+        axis=0,
+    )
     column_blocks = column_group.reshape(-1, tile_size, feature_count)
     row_blocks = row_group.reshape(-1, tile_size, feature_count)
     row_span = row_blocks.shape[0]

time: 882 us -> 743 us (0.84)
  waiting for transfers between devices: 548 us -> 282 us
  blocking collectives: 114 us -> 222 us
  starting transfers between devices: 17.4 us -> 34.2 us
    all_gather x2 -> x0, waiting for transfers between devices: 244 us -> none  [aggregate(): row_group = lax.all_gather(node_data, 'col', axis=0, tiled=True)]
    all_gather x2, blocking collectives: 37.8 us -> 143 us  [stacked_from(): blocks = lax.all_gather(blocks, axes[k], axis=0, tiled=True)]
    reduce_scatter x4, waiting for transfers between devices: 99 us -> 71.6 us  [sum_in_order(): blocks = lax.psum_scatter(blocks, axes[k], scatter_dimension=0, tiled=True)]
    all_to_all x0 -> x2, starting transfers between devices: none -> 17.3 us  [aggregate(): lax.all_to_all(jnp.stack([node_data for _ in range(lax.axis_size('col'))]...]
    all_to_all x2, waiting for transfers between devices: 0.01 us -> 10.2 us  [sent_and_summed(): lax.all_to_all(split_up(array, dim, length), axis, 0, 0, tiled=True)]
    unnamed x10 -> x8, waiting for transfers between devices: 181 us -> 178 us
  transfers between devices with their start and end apart: 11 -> 11, of which waited for: 9 -> 8; matrix products, arithmetic and copies ran while one was open for 21% -> 24% of each run, Pallas kernels for 0% -> 0%
where the time goes in v1:
time: 743 us; the launch traced here: 742 us
  waiting for transfers between devices  282 us (38%)
  blocking collectives  222 us (30%)
  other arithmetic  79.2 us (11%)
  local copies, waits for them, and re-layouts  72.4 us (10%)
  matrix products  37.5 us (5%)
  starting transfers between devices  34.2 us (5%)
  between operations  14.4 us (2%)
    unnamed x8, waiting for transfers between devices  178 us
    all_gather x2, blocking collectives, stacked_from(): blocks = lax.all_gather(blocks, axes[k], axis=0, tiled=True)  143 us
    unnamed x1, blocking collectives  78.8 us
    reduce_scatter x4, waiting for transfers between devices, sum_in_order(): blocks = lax.psum_scatter(blocks, axes[k], scatter_dimension=0, tiled=True)  71.6 us
    scatter-add x2, other arithmetic, aggregate(): row_partial = jnp.zeros((row_span, tile_size, feature_count), jnp.float32...  36.6 us
    scatter-add x2, other arithmetic, aggregate(): column_partial = jnp.zeros((column_span, tile_size, feature_count), jnp.f...  23.3 us
    all_gather x2, waiting for transfers between devices, stacked_from(): blocks = lax.all_gather(blocks, axes[k], axis=0, tiled=True)  22.1 us
    mul x2, local copies, waits for them, and re-layouts, aggregate(): mirror_terms * live  17.9 us
  transfers between devices with their start and end apart: 11, of which 8 were waited for; matrix products, arithmetic and copies ran while one was open for 24% of the time, Pallas kernels for 0%

profile of v1, /device:TPU:8, one launch (start us, length us, event | category | flops | bytes accessed | tf_op | source)
XLA Modules:
  0.0 741.6 jit_solution(11563763875444608248)
XLA Ops:
  10.6 9.1 %all-to-all-start.1 = ((bf16[32,256,256]{2,1,0:T(8,128)(2,1)}), bf16[32,256,256]{2,1,0:T(8,128)(2,1)}, u32[]{:S(2)}, u32[]{:S(2)}) async-start(bf16[32,256,256]{2,1,0:T(8,128)(2,1)} %stack.4), calls=%async_computation.1 | async-start | bytes 8388608 | tf_op jit(solution)/shard_map/all_to_all | solution.py:66
  19.7 77.1 %all-gather = bf16[1024,256]{1,0:T(8,128)(2,1)} all-gather(bf16[256,256]{1,0:T(8,128)(2,1)S(1)} %copy-done.2), channel_id=2, replica_groups=mesh['row_0'=4,'row_1'=2,'col'=32] {'row_0'}, dimensions={0}, use_global_device_ids=true | all-gather | bytes 655360 | tf_op jit(solution)/shard_map/all_gather | solution.py:21
  96.9 9.4 %all-gather.5.cloned.1.call-done = bf16[8,256,256]{2,1,0:T(8,128)(2,1)} async-done(((bf16[4,256,256]{2,1,0:T(8,128)(2,1)}), bf16[8,256,256]{2,1,0:T(8,128)(2,1)}) %all-gather.5.cloned.1.call-update) | async-done | bytes 1048592 | tf_op jit(solution)/shard_map/all_gather | solution.py:21
  110.4 8.6 %multiply_bitcast_fusion.3 = f32[32,256,256]{1,2,0:T(8,128)} fusion(f32[32]{0:T(128)S(1)} %bitcast_convert_fusion, bf16[32,256,256]{2,1,0:T(8,128)(2,1)} %param.14, bf16[32,256,256]{2,1,0:T(8,128)(2,1)} %gather_fusion, pred[32]{0:T(512)(128)(4,1)S(1)} %get-tuple-element.13), kind=kOutput, calls=%fused_computation.13 | convolution fusion | flops 1077936128 | bytes 16777376 | tf_op jit(solution)/shard_map/tnm,tmf->tnf/dot_general | solution.py:84
  119.0 9.0 %copy.39 = f32[32,256,256]{2,1,0:T(8,128)} copy(f32[32,256,256]{1,2,0:T(8,128)} %multiply_bitcast_fusion.3) | data formatting | bytes 16777216 | tf_op jit(solution)/shard_map/mul | solution.py:94
  128.0 4.2 broadcast.115.clone
  132.2 18.3 %scatter_fusion = f32[32,256,256]{2,1,0:T(8,128)} fusion(f32[32,256,256]{2,1,0:T(8,128)} %broadcast.115.clone, s32[32]{0:T(128)S(1)} %get-tuple-element.16, f32[32,256,256]{2,1,0:T(8,128)} %copy.39), kind=kCustom, calls=%fused_computation.4 | custom fusion | flops 2097152 | bytes 25165952 | tf_op jit(solution)/shard_map/scatter-add | solution.py:94
  150.5 5.9 convert_element_type.70
  156.4 8.3 %all-to-all-start = ((bf16[32,256,256]{2,1,0:T(8,128)(2,1)}), bf16[32,256,256]{2,1,0:T(8,128)(2,1)}, u32[]{:S(2)}, u32[]{:S(2)}) async-start(bf16[32,256,256]{2,1,0:T(8,128)(2,1)} %convert_element_type.70), calls=%async_computation | async-start | bytes 8388608 | tf_op jit(solution)/shard_map/all_to_all | solution.py:40
  164.8 5.0 gather_fusion.1
  169.8 8.6 %multiply_bitcast_fusion.2 = f32[32,256,256]{1,2,0:T(8,128)} fusion(f32[32]{0:T(128)S(1)} %bitcast_convert_fusion, bf16[32,256,256]{2,1,0:T(8,128)(2,1)} %param.14, bf16[32,256,256]{2,1,0:T(8,128)(2,1)} %gather_fusion.1, pred[32]{0:T(512)(128)(4,1)S(1)} %get-tuple-element.8), kind=kOutput, calls=%fused_computation.11 | convolution fusion | flops 1077936128 | bytes 16777376 | tf_op jit(solution)/shard_map/tmn,tmf->tnf/dot_general | solution.py:87
  178.4 9.0 %copy.41 = f32[32,256,256]{2,1,0:T(8,128)} copy(f32[32,256,256]{1,2,0:T(8,128)} %multiply_bitcast_fusion.2) | data formatting | bytes 16777216 | tf_op jit(solution)/shard_map/mul | solution.py:99
  187.5 11.6 %scatter_fusion.1 = f32[8,256,256]{2,1,0:T(8,128)S(1)} fusion(f32[8,256,256]{2,1,0:T(8,128)S(1)} %broadcast.118.clone, s32[32]{0:T(128)S(1)} %get-tuple-element.15, f32[32,256,256]{2,1,0:T(8,128)} %copy.41), kind=kCustom, calls=%fused_computation.5 | custom fusion | flops 2097152 | bytes 25165952 | tf_op jit(solution)/shard_map/scatter-add | solution.py:99
  200.4 14.7 %reduce-scatter.5.cloned.1.call-done = bf16[4,256,256]{2,1,0:T(8,128)(2,1)} async-done(((bf16[8,256,256]{2,1,0:T(8,128)(2,1)}), bf16[4,256,256]{2,1,0:T(8,128)(2,1)}) %reduce-scatter.5.cloned.1.call-update) | async-done | bytes 524304 | tf_op jit(solution)/shard_map/reduce_scatter | solution.py:50
  215.1 10.2 %all-to-all-done = bf16[32,256,256]{2,1,0:T(8,128)(2,1)} async-done(((bf16[32,256,256]{2,1,0:T(8,128)(2,1)}), bf16[32,256,256]{2,1,0:T(8,128)(2,1)}, u32[]{:S(2)}, u32[]{:S(2)}) %all-to-all-start) | async-done | bytes 4194336 | tf_op jit(solution)/shard_map/all_to_all | solution.py:40
  228.2 18.1 %reduce-scatter.7.cloned.1.call-done = bf16[1,256,256]{2,1,0:T(8,128)(2,1)} async-done(((bf16[4,256,256]{2,1,0:T(8,128)(2,1)}), bf16[1,256,256]{2,1,0:T(8,128)(2,1)}) %reduce-scatter.7.cloned.1.call-update) | async-done | bytes 131088 | tf_op jit(solution)/shard_map/reduce_scatter | solution.py:50
  250.8 8.2 %all-to-all-start.3 = ((bf16[32,256,256]{2,1,0:T(8,128)(2,1)}), bf16[32,256,256]{2,1,0:T(8,128)(2,1)}, u32[]{:S(2)}, u32[]{:S(2)}) async-start(bf16[32,256,256]{2,1,0:T(8,128)(2,1)} %stack.5), calls=%async_computation.5 | async-start | bytes 8388608 | tf_op jit(solution)/shard_map/all_to_all | solution.py:66
  259.0 66.0 %all-gather.1 = bf16[1024,256]{1,0:T(8,128)(2,1)} all-gather(bf16[256,256]{1,0:T(8,128)(2,1)S(1)} %convolution_convert_fusion), channel_id=3, replica_groups=mesh['row_0'=4,'row_1'=2,'col'=32] {'row_0'}, dimensions={0}, use_global_device_ids=true | all-gather | bytes 655360 | tf_op jit(solution)/shard_map/all_gather | solution.py:21
  325.1 12.7 %all-gather.7.cloned.1.call-done = bf16[8,256,256]{2,1,0:T(8,128)(2,1)} async-done(((bf16[4,256,256]{2,1,0:T(8,128)(2,1)}), bf16[8,256,256]{2,1,0:T(8,128)(2,1)}) %all-gather.7.cloned.1.call-update) | async-done | bytes 1048592 | tf_op jit(solution)/shard_map/all_gather | solution.py:21
  341.9 8.6 %multiply_bitcast_fusion.1 = f32[32,256,256]{1,2,0:T(8,128)} fusion(f32[32]{0:T(128)S(1)} %bitcast_convert_fusion, bf16[32,256,256]{2,1,0:T(8,128)(2,1)} %param.14, bf16[32,256,256]{2,1,0:T(8,128)(2,1)} %gather_fusion.2, pred[32]{0:T(512)(128)(4,1)S(1)} %get-tuple-element.13), kind=kOutput, calls=%fused_computation.10 | convolution fusion | flops 1077936128 | bytes 16777376 | tf_op jit(solution)/shard_map/tnm,tmf->tnf/dot_general | solution.py:84
  350.5 9.0 %copy.45 = f32[32,256,256]{2,1,0:T(8,128)} copy(f32[32,256,256]{1,2,0:T(8,128)} %multiply_bitcast_fusion.1) | data formatting | bytes 16777216 | tf_op jit(solution)/shard_map/mul | solution.py:94
  363.6 18.3 %scatter_fusion.2 = f32[32,256,256]{2,1,0:T(8,128)} fusion(f32[32,256,256]{2,1,0:T(8,128)} %broadcast.115, s32[32]{0:T(128)S(1)} %get-tuple-element.16, f32[32,256,256]{2,1,0:T(8,128)} %copy.45), kind=kCustom, calls=%fused_computation.6 | custom fusion | flops 2097152 | bytes 25165952 | tf_op jit(solution)/shard_map/scatter-add | solution.py:94
  381.9 5.9 convert_element_type.81
  387.8 8.3 %all-to-all-start.2 = ((bf16[32,256,256]{2,1,0:T(8,128)(2,1)}), bf16[32,256,256]{2,1,0:T(8,128)(2,1)}, u32[]{:S(2)}, u32[]{:S(2)}) async-start(bf16[32,256,256]{2,1,0:T(8,128)(2,1)} %convert_element_type.81), calls=%async_computation.4 | async-start | bytes 8388608 | tf_op jit(solution)/shard_map/all_to_all | solution.py:40
  396.2 5.0 gather_fusion.3
  401.2 8.6 %multiply_bitcast_fusion = f32[32,256,256]{1,2,0:T(8,128)} fusion(f32[32]{0:T(128)S(1)} %bitcast_convert_fusion, bf16[32,256,256]{2,1,0:T(8,128)(2,1)} %param.14, bf16[32,256,256]{2,1,0:T(8,128)(2,1)} %gather_fusion.3, pred[32]{0:T(512)(128)(4,1)S(1)} %get-tuple-element.8), kind=kOutput, calls=%fused_computation.8 | convolution fusion | flops 1077936128 | bytes 16777376 | tf_op jit(solution)/shard_map/tmn,tmf->tnf/dot_general | solution.py:87
  409.8 9.0 %copy.47 = f32[32,256,256]{2,1,0:T(8,128)} copy(f32[32,256,256]{1,2,0:T(8,128)} %multiply_bitcast_fusion) | data formatting | bytes 16777216 | tf_op jit(solution)/shard_map/mul | solution.py:99
  418.9 11.6 %scatter_fusion.3 = f32[8,256,256]{2,1,0:T(8,128)S(1)} fusion(f32[8,256,256]{2,1,0:T(8,128)S(1)} %broadcast.118, s32[32]{0:T(128)S(1)} %get-tuple-element.15, f32[32,256,256]{2,1,0:T(8,128)} %copy.47), kind=kCustom, calls=%fused_computation.7 | custom fusion | flops 2097152 | bytes 25165952 | tf_op jit(solution)/shard_map/scatter-add | solution.py:99
  432.9 13.6 %reduce-scatter.9.cloned.1.call-done = bf16[4,256,256]{2,1,0:T(8,128)(2,1)} async-done(((bf16[8,256,256]{2,1,0:T(8,128)(2,1)}), bf16[4,256,256]{2,1,0:T(8,128)(2,1)}) %reduce-scatter.9.cloned.1.call-update) | async-done | bytes 524304 | tf_op jit(solution)/shard_map/reduce_scatter | solution.py:50
  446.6 78.8 %all-reduce.1 = f32[256]{0:T(256)S(1)} all-reduce(f32[256]{0:T(256)S(1)} %broadcast_multiply_fusion), channel_id=9, replica_groups=mesh['row_0'=4,'row_1'=2,'col'=32] {'row_0','row_1','col'}, use_global_device_ids=true, to_apply=%region_12.15.clone | all-reduce | flops 256 | bytes 2048
  526.0 178.0 %all-reduce.4.cloned.1.call-done = f32[256,256]{1,0:T(8,128)} async-done(((f32[256,256]{1,0:T(8,128)}), f32[256,256]{1,0:T(8,128)}) %all-reduce.4.cloned.1.call-update) | async-done | bytes 262160
  708.0 25.2 %reduce-scatter.11.cloned.1.call-done = bf16[1,256,256]{2,1,0:T(8,128)(2,1)} async-done(((bf16[4,256,256]{2,1,0:T(8,128)(2,1)}), bf16[1,256,256]{2,1,0:T(8,128)(2,1)}) %reduce-scatter.11.cloned.1.call-update) | async-done | bytes 131088 | tf_op jit(solution)/shard_map/reduce_scatter | solution.py:50
  (58 shorter events, 33.3 us)
Async XLA Ops:
  7.2 239.1 %copy-start = (bf16[256,256]{1,0:T(8,128)(2,1)S(1)}, bf16[256,256]{1,0:T(8,128)(2,1)}, u32[]{:S(2)}) copy-start(bf16[256,256]{1,0:T(8,128)(2,1)} %param.11) | copy-start | bytes 393220
  10.6 9.1 %copy-start.2 = (bf16[256,256]{1,0:T(8,128)(2,1)S(1)}, bf16[256,256]{1,0:T(8,128)(2,1)}, u32[]{:S(2)}) copy-start(bf16[256,256]{1,0:T(8,128)(2,1)} %param.10) | copy-start | bytes 393220
  10.6 86.3 %copy-start.4 = (s32[32,2]{0,1:T(2,128)S(1)}, s32[32,2]{0,1:T(2,128)}, u32[]{:S(2)}) copy-start(s32[32,2]{0,1:T(2,128)} %param.15) | copy-start | bytes 772
  10.6 145.8 %all-to-all-start.1 = ((bf16[32,256,256]{2,1,0:T(8,128)(2,1)}), bf16[32,256,256]{2,1,0:T(8,128)(2,1)}, u32[]{:S(2)}, u32[]{:S(2)}) async-start(bf16[32,256,256]{2,1,0:T(8,128)(2,1)} %stack.4), calls=%async_computation.1 | async-start | bytes 8388608 | tf_op jit(solution)/shard_map/all_to_all | solution.py:66
  19.6 86.7 %all-gather.5.cloned.1.call-start = ((), (), s32[]{:S(2)}) async-start(), calls=%async_computation.8 | async-start | bytes 1572864 | tf_op jit(solution)/shard_map/all_gather | solution.py:21
  156.4 69.0 %all-to-all-start = ((bf16[32,256,256]{2,1,0:T(8,128)(2,1)}), bf16[32,256,256]{2,1,0:T(8,128)(2,1)}, u32[]{:S(2)}, u32[]{:S(2)}) async-start(bf16[32,256,256]{2,1,0:T(8,128)(2,1)} %convert_element_type.70), calls=%async_computation | async-start | bytes 8388608 | tf_op jit(solution)/shard_map/all_to_all | solution.py:40
  164.7 50.4 %reduce-scatter.5.cloned.1.call-start = ((), (), s32[]{:S(2)}) async-start(), calls=%async_computation.9 | async-start | bytes 1572864 | tf_op jit(solution)/shard_map/reduce_scatter | solution.py:50
  199.3 47.0 %copy-start.5 = (bf16[256,256]{1,0:T(8,128)(2,1)S(1)}, bf16[256,256]{1,0:T(8,128)(2,1)}, u32[]{:S(2)}) copy-start(bf16[256,256]{1,0:T(8,128)(2,1)} %param.13) | copy-start | bytes 393220
  199.3 47.0 %copy-start.6 = (f32[256]{0:T(256)S(1)}, f32[256]{0:T(256)}, u32[]{:S(2)}) copy-start(f32[256]{0:T(256)} %param.12) | copy-start | bytes 3076
  200.4 45.9 %reduce-scatter.7.cloned.1.call-start = ((), (), s32[]{:S(2)}) async-start(), calls=%async_computation.10 | async-start | bytes 655360 | tf_op jit(solution)/shard_map/reduce_scatter | solution.py:50
  250.8 137.0 %all-to-all-start.3 = ((bf16[32,256,256]{2,1,0:T(8,128)(2,1)}), bf16[32,256,256]{2,1,0:T(8,128)(2,1)}, u32[]{:S(2)}, u32[]{:S(2)}) async-start(bf16[32,256,256]{2,1,0:T(8,128)(2,1)} %stack.5), calls=%async_computation.5 | async-start | bytes 8388608 | tf_op jit(solution)/shard_map/all_to_all | solution.py:66
  259.0 78.8 %all-gather.7.cloned.1.call-start = ((), (), s32[]{:S(2)}) async-start(), calls=%async_computation.11 | async-start | bytes 1572864 | tf_op jit(solution)/shard_map/all_gather | solution.py:21
  387.8 317.3 %all-to-all-start.2 = ((bf16[32,256,256]{2,1,0:T(8,128)(2,1)}), bf16[32,256,256]{2,1,0:T(8,128)(2,1)}, u32[]{:S(2)}, u32[]{:S(2)}) async-start(bf16[32,256,256]{2,1,0:T(8,128)(2,1)} %convert_element_type.81), calls=%async_computation.4 | async-start | bytes 8388608 | tf_op jit(solution)/shard_map/all_to_all | solution.py:40
  396.1 50.4 %reduce-scatter.9.cloned.1.call-start = ((), (), s32[]{:S(2)}) async-start(), calls=%async_computation.12 | async-start | bytes 1572864 | tf_op jit(solution)/shard_map/reduce_scatter | solution.py:50
  430.6 1.3 copy-start.3
  430.7 304.1 %copy-start.1 = (bf16[256,256]{1,0:T(8,128)(2,1)S(1)}, bf16[256,256]{1,0:T(8,128)(2,1)}, u32[]{:S(2)}) copy-start(bf16[256,256]{1,0:T(8,128)(2,1)} %param.11) | copy-start | bytes 393220
  431.8 272.1 %all-reduce.4.cloned.1.call-start = ((), (), s32[]{:S(2)}) async-start(), calls=%async_computation.14 | async-start | bytes 524288
  432.8 300.4 %reduce-scatter.11.cloned.1.call-start = ((), (), s32[]{:S(2)}) async-start(), calls=%async_computation.13 | async-start | bytes 655360 | tf_op jit(solution)/shard_map/reduce_scatter | solution.py:50
Sparse Core Ops, SparseCore 0:
  96.9 9.3 all-gather.4
  200.5 14.5 reduce-scatter.4
  217.8 28.4 reduce-scatter.6
  325.2 12.5 all-gather.6
  431.9 14.5 reduce-scatter.8
  451.8 252.0 all-reduce.3
  706.4 26.7 reduce-scatter.10
